TPU v7x, 128 devices: a whole 4x4x4 slice. The times are simulated.
128 devices in a mesh: prow: 16 (over z, x), pcol: 8 (over y, core).
Axes of the slice: x: 4, y: 4, z: 4, core: 2. Of those that a mesh axis runs over, the one named last changes fastest.
Arguments:
- kernel_tiles: float32 [4, 16, 256, 8, 8, 256], P(None, 'prow', None, None, 'pcol'), may hold values from 0 to 11, as said below
Outputs:
- factored: float32 [4, 16, 256, 8, 8, 256], P(None, 'prow', None, None, 'pcol')
Inputs may be any that keep to these rules, and one draw needn't show every extreme that they name: kernel_tiles is a symmetric positive definite matrix in the stated layout: a product of two exponential covariances of locations and times, scaled per point, plus a diagonal term of at least 0.5.
All inputs are finite; a program needn't handle non-finite values.
Results may differ from a plain program's by a relative error of at most 0.000061.
Values sent between devices are 32-bit elements; how exact they have to be, the bound alone decides.
A program may use at most 128 MiB of HBM per device.

v0:
```python
import jax
import jax.numpy as jnp
from jax import lax
from jax.sharding import PartitionSpec as P

highest = lax.Precision.HIGHEST


def picked(shard, axis, root):
    return lax.dynamic_index_in_dim(lax.all_gather(shard, axis), root, 0, keepdims=False)


def from_root(shard, axis, root):
    mine = lax.axis_index(axis) == root
    return lax.psum(jnp.where(mine, shard, jnp.zeros_like(shard)), axis)


def tile_solve(factor, tile_rows):
    tile_count, tile_width, _ = tile_rows.shape
    flat_rows = tile_rows.reshape(tile_count * tile_width, tile_width)
    solved = jax.scipy.linalg.solve_triangular(factor, flat_rows.T, lower=True)
    return solved.T.reshape(tile_count, tile_width, tile_width)


def factor_panel(local_block, panel_index, global_rows):
    procs_row = lax.axis_size("prow")
    procs_col = lax.axis_size("pcol")
    tile_row = panel_index // procs_row
    tile_col = panel_index // procs_col
    factor = jnp.linalg.cholesky(local_block[tile_row, :, tile_col, :])
    factor = picked(factor, "prow", panel_index % procs_row)
    solved = tile_solve(factor, local_block[:, :, tile_col, :])
    lower_rows = (global_rows > panel_index)[:, None, None]
    diag_rows = (global_rows == panel_index)[:, None, None]
    panel = jnp.where(lower_rows, solved, jnp.where(diag_rows, factor[None], jnp.float32(0.0)))
    row_panel = picked(panel, "pcol", panel_index % procs_col)
    return (panel, row_panel)


def column_tiles(row_panel):
    procs_row = lax.axis_size("prow")
    tile_width = row_panel.shape[1]
    procs_col = lax.axis_size("pcol")
    multiple = procs_row // procs_col
    col_index = lax.axis_index("pcol")
    received = []
    for owner_step in range(multiple):
        received.append(from_root(row_panel, "prow", col_index + owner_step * procs_col))
    stacked = jnp.stack(received, axis=1)
    return stacked.reshape(-1, tile_width, tile_width)


def trailing(local_block, lead, global_rows, global_cols, row_panel, col_panel):
    update = jnp.einsum("arn,csn->arcs", row_panel, col_panel, precision=highest)
    active = (global_rows > lead)[:, None, None, None] & (global_cols > lead)[None, None, :, None]
    return jnp.where(active, local_block - update, local_block)


def write_panel(local_block, panel_index, panel, global_rows, global_cols):
    in_column = (global_cols == panel_index)[None, None, :, None]
    result = jnp.where(in_column, panel[:, :, None, :], local_block)
    upper = (global_rows == panel_index)[:, None, None, None] & (global_cols > panel_index)[
        None, None, :, None
    ]
    return jnp.where(upper, jnp.float32(0.0), result)


def shards(kernel_tiles):
    row_count, _, tile_width, col_count, _, _ = kernel_tiles.shape
    local_block = kernel_tiles.reshape(row_count, tile_width, col_count, tile_width)
    global_rows = jnp.arange(row_count, dtype=jnp.int32) * lax.axis_size("prow") + lax.axis_index(
        "prow"
    )
    global_cols = jnp.arange(col_count, dtype=jnp.int32) * lax.axis_size("pcol") + lax.axis_index(
        "pcol"
    )
    panel_zero, rows_zero = factor_panel(local_block, 0, global_rows)
    cols_zero = column_tiles(rows_zero)
    result = trailing(local_block, 0, global_rows, global_cols, rows_zero, cols_zero)
    result = write_panel(result, 0, panel_zero, global_rows, global_cols)
    panel_one, rows_one = factor_panel(result, 1, global_rows)
    cols_one = column_tiles(rows_one)
    result = trailing(result, 1, global_rows, global_cols, rows_one, cols_one)
    result = write_panel(result, 1, panel_one, global_rows, global_cols)
    return result.reshape(kernel_tiles.shape)


def solution(mesh):
    in_specs = (P(None, "prow", None, None, "pcol", None),)
    out_specs = P(None, "prow", None, None, "pcol", None)
    return jax.shard_map(shards, mesh=mesh, in_specs=in_specs, out_specs=out_specs, check_vma=False)
```

profile of v0, /device:TPU:88, one launch (start us, length us, event | category | flops | bytes accessed | tf_op | source)
XLA Modules:
  0.0 608.7 jit_solution(7833220030949401913)
XLA Ops:
  6.5 20.5 %copy.31 = f32[4,1,256,8,1,256]{2,5,3,0,4,1:T(8,128)} copy(f32[4,1,256,8,1,256]{5,4,3,2,1,0:T(1,128)} %param.4) | data formatting | bytes 16777216 | tf_op args[0]
  29.2 11.7 %cholesky.130 = f32[128,128]{1,0:T(8,128)S(1)} custom-call(f32[128,128]{1,0:T(8,128)S(1)} %cholesky.194), custom_call_target="Cholesky" | custom-call | tf_op jit(solution)/shard_map/jit(cholesky)/cholesky | solution.py:30
  41.0 9.8 %custom-call.13 = f32[1,128,128]{1,2,0:T(8,128)S(1)} custom-call(f32[1,128,128]{2,1,0:T(8,128)S(1)} %get-tuple-element.62), custom_call_target="InvertDiagBlocksLowerTriangular" | custom-call | tf_op jit(solution)/shard_map/jit(cholesky)/cholesky | solution.py:30
  51.3 11.7 %cholesky.147 = f32[128,128]{1,0:T(8,128)S(1)} custom-call(f32[128,128]{1,0:T(8,128)S(1)} %convolution_subtract_fusion.3), custom_call_target="Cholesky" | custom-call | tf_op jit(solution)/shard_map/jit(cholesky)/cholesky | solution.py:30
  66.2 1.3 slice.70
  68.2 50.4 %all-gather.11.cloned.1.call-done = f32[4096,256]{1,0:T(8,128)} async-done(((f32[256,256]{1,0:T(8,128)}), f32[4096,256]{1,0:T(8,128)}) %all-gather.11.cloned.1.call-update) | async-done | bytes 4194320 | tf_op jit(solution)/shard_map/all_gather | solution.py:10
  119.6 3.8 while.4
  120.3 1.3 bitcast_dynamic-update-slice_fusion.4
  122.2 1.3 bitcast_dynamic-update-slice_fusion.4
  123.5 19.7 %custom-call.14 = f32[2,128,128]{1,2,0:T(8,128)S(1)} custom-call(f32[2,128,128]{2,1,0:T(8,128)S(1)} %get-tuple-element.21), custom_call_target="InvertDiagBlocksLowerTriangular" | custom-call | tf_op jit(solution)/shard_map/jit(_solve_triangular)/triangular_solve | solution.py:21
  146.8 47.9 %all-gather.7.cloned.1.call-done = f32[8,4,256,256]{3,2,1,0:T(8,128)} async-done(((f32[1,4,256,256]{3,2,1,0:T(8,128)}), f32[8,4,256,256]{3,2,1,0:T(8,128)}) %all-gather.7.cloned.1.call-update) | async-done | bytes 8388624 | tf_op jit(solution)/shard_map/all_gather | solution.py:10
  194.7 2.8 fusion.9
  198.1 90.8 %all-reduce.8.cloned.1.call-done = (f32[4,1,256,256]{3,2,0,1:T(8,128)}, f32[4,1,256,256]{3,2,0,1:T(8,128)}) async-done(((f32[4,1,256,256]{3,2,0,1:T(8,128)}, f32[4,1,256,256]{3,2,0,1:T(8,128)}), (f32[4,1,256,256]{3,2,0,1:T(8,128)}, f32[4,1,256,256]{3,2,0,1:T(8,128)})) %all-reduce.8.cloned.1.call-update) | async-done | bytes 2097168 | tf_op jit(solution)/shard_map/psum | solution.py:15
  288.9 1.7 pad_maximum_fusion
  290.7 11.1 %fusion.1 = f32[4,256,8,256]{1,3,2,0:T(8,128)S(1)} fusion(f32[4,256,256]{1,2,0:T(8,128)S(1)} %copy.36, pred[8]{0:T(512)(128)(4,1)S(1)} %broadcast_compare_fusion, pred[4,8]{1,0:T(4,128)(4,1)S(1)} %get-tuple-element.66, pred[4,8]{1,0:T(4,128)(4,1)S(1)} %get-tuple-element.65, f32[8,256,256,1]{2,1,0,3:T(8,128)S(1)} %bitcast.131, ...), kind=kOutput, calls=%fused_computation.7 | convolution fusion | flops 6450839552 | bytes 20971592 | tf_op jit(solution)/shard_map/arn,csn->arcs/dot_general | solution.py:54
  301.8 3.4 copy-done
  306.4 11.7 %cholesky.164 = f32[128,128]{1,0:T(8,128)S(1)} custom-call(f32[128,128]{1,0:T(8,128)S(1)} %cholesky.197), custom_call_target="Cholesky" | custom-call | tf_op jit(solution)/shard_map/jit(cholesky)/cholesky | solution.py:30
  318.1 9.8 %custom-call.15 = f32[1,128,128]{1,2,0:T(8,128)S(1)} custom-call(f32[1,128,128]{2,1,0:T(8,128)S(1)} %get-tuple-element.58), custom_call_target="InvertDiagBlocksLowerTriangular" | custom-call | tf_op jit(solution)/shard_map/jit(cholesky)/cholesky | solution.py:30
  328.4 11.7 %cholesky.181 = f32[128,128]{1,0:T(8,128)S(1)} custom-call(f32[128,128]{1,0:T(8,128)S(1)} %convolution_subtract_fusion.2), custom_call_target="Cholesky" | custom-call | tf_op jit(solution)/shard_map/jit(cholesky)/cholesky | solution.py:30
  343.5 1.3 slice.73
  345.5 50.6 %all-gather.13.cloned.1.call-done = f32[4096,256]{1,0:T(8,128)} async-done(((f32[256,256]{1,0:T(8,128)}), f32[4096,256]{1,0:T(8,128)}) %all-gather.13.cloned.1.call-update) | async-done | bytes 4194320 | tf_op jit(solution)/shard_map/all_gather | solution.py:10
  397.1 4.0 while.5
  398.0 1.3 bitcast_dynamic-update-slice_fusion.5
  399.9 1.3 bitcast_dynamic-update-slice_fusion.5
  401.2 19.7 %custom-call.16 = f32[2,128,128]{1,2,0:T(8,128)S(1)} custom-call(f32[2,128,128]{2,1,0:T(8,128)S(1)} %get-tuple-element.22), custom_call_target="InvertDiagBlocksLowerTriangular" | custom-call | tf_op jit(solution)/shard_map/jit(_solve_triangular)/triangular_solve | solution.py:21
  423.2 1.3 select_select_fusion
  424.5 47.9 %all-gather.9.cloned.1.call-done = f32[8,4,256,256]{3,2,1,0:T(8,128)} async-done(((f32[1,4,256,256]{3,2,1,0:T(8,128)}), f32[8,4,256,256]{3,2,1,0:T(8,128)}) %all-gather.9.cloned.1.call-update) | async-done | bytes 8388624 | tf_op jit(solution)/shard_map/all_gather | solution.py:10
  472.4 2.8 fusion.7
  475.7 91.1 %all-reduce.6.cloned.1.call-done = (f32[4,1,256,256]{3,2,0,1:T(8,128)}, f32[4,1,256,256]{3,2,0,1:T(8,128)}) async-done(((f32[4,1,256,256]{3,2,0,1:T(8,128)}, f32[4,1,256,256]{3,2,0,1:T(8,128)}), (f32[4,1,256,256]{3,2,0,1:T(8,128)}, f32[4,1,256,256]{3,2,0,1:T(8,128)})) %all-reduce.6.cloned.1.call-update) | async-done | bytes 2097168 | tf_op jit(solution)/shard_map/psum | solution.py:15
  566.8 1.7 pad_maximum_fusion.1
  568.6 12.4 %fusion.4 = f32[4,1,256,8,1,256]{2,5,3,0,4,1:T(8,128)} fusion(f32[4,256,8,256]{1,3,2,0:T(8,128)} %copy-done, f32[4,256,256]{1,2,0:T(8,128)S(1)} %copy.44, pred[8]{0:T(512)(128)(4,1)S(1)} %broadcast_compare_fusion.4, pred[4,8]{1,0:T(4,128)(4,1)S(1)} %get-tuple-element.64, pred[4,8]{1,0:T(4,128)(4,1)S(1)} %get-tuple-element.63, ...), kind=kOutput, calls=%fused_computation.10 | convolution fusion | flops 6450839552 | bytes 20971592 | tf_op jit(solution)/shard_map/arn,csn->arcs/dot_general | solution.py:54
  581.1 20.5 %copy.48 = f32[4,1,256,8,1,256]{5,4,3,2,1,0:T(1,128)} copy(f32[4,1,256,8,1,256]{2,5,3,0,4,1:T(8,128)} %fusion.4) | data formatting | bytes 16777216 | tf_op jit(solution)/shard_map/reshape | solution.py:85
  (78 shorter events, 21.6 us)
Async XLA Ops:
  6.5 112.0 %all-gather.11.cloned.1.call-start = ((), (), s32[]{:S(2)}) async-start(), calls=%async_computation.2 | async-start | bytes 4456448 | tf_op jit(solution)/shard_map/all_gather | solution.py:10
  65.6 129.0 %all-gather.7.cloned.1.call-start = ((), (), s32[]{:S(2)}) async-start(), calls=%async_computation | async-start | bytes 9437184 | tf_op jit(solution)/shard_map/all_gather | solution.py:10
  146.7 142.2 %all-reduce.8.cloned.1.call-start = ((), (), s32[]{:S(2)}) async-start(), calls=%async_computation.5 | async-start | bytes 4194304 | tf_op jit(solution)/shard_map/psum | solution.py:15
  197.4 198.7 %all-gather.13.cloned.1.call-start = ((), (), s32[]{:S(2)}) async-start(), calls=%async_computation.3 | async-start | bytes 4456448 | tf_op jit(solution)/shard_map/all_gather | solution.py:10
  301.8 3.4 copy-start
  343.4 128.9 %all-gather.9.cloned.1.call-start = ((), (), s32[]{:S(2)}) async-start(), calls=%async_computation.1 | async-start | bytes 9437184 | tf_op jit(solution)/shard_map/all_gather | solution.py:10
  424.4 142.4 %all-reduce.6.cloned.1.call-start = ((), (), s32[]{:S(2)}) async-start(), calls=%async_computation.4 | async-start | bytes 4194304 | tf_op jit(solution)/shard_map/psum | solution.py:15
Sparse Core Ops, SparseCore 0:
  65.8 52.7 all-gather.10
  146.9 47.7 all-gather.6
  198.1 90.7 all-reduce.7
  343.6 52.5 all-gather.12
  424.6 47.7 all-gather.8
  476.0 90.7 all-reduce.5
where the time goes:
time: 621 us; the launch traced here: 609 us
  waiting for transfers between devices  379 us (61%)
  other arithmetic  125 us (20%)
  local copies, waits for them, and re-layouts  58.9 us (9%)
  matrix products  28.1 us (5%)
  between operations  16.5 us (3%)
    all_gather x4, waiting for transfers between devices, picked(): lax.all_gather(shard, axis)  197 us
    psum x2, waiting for transfers between devices, from_root(): return lax.psum(jnp.where(mine, shard, jnp.zeros_like(shard)), axis)  182 us
    another operation x13, other arithmetic, factor_panel(): factor = jnp.linalg.cholesky(local_block[tile_row, :, tile_col, :])  68.6 us
    another operation x3, other arithmetic, tile_solve(): solved = jax.scipy.linalg.solve_triangular(factor, flat_rows.T, lower=True)  39.4 us
    unnamed x3, local copies, waits for them, and re-layouts  23.9 us
    dot_general x2, matrix products, trailing(): jnp.einsum('arn,csn->arcs', row_panel, col_panel, precision=highest)  23.5 us
    reshape x1, local copies, waits for them, and re-layouts, shards(): return result.reshape(kernel_tiles.shape)  20.5 us
  transfers between devices with their start and end apart: 6, of which 6 were waited for; matrix products, arithmetic and copies ran while one was open for 1% of the time, Pallas kernels for 0%

commit v1 on v0

v1 whole, which is shorter than its diff:
```python
import functools

import jax
import jax.numpy as jnp
from jax import lax
from jax.experimental import pallas as pl
from jax.experimental.pallas import tpu as pltpu
from jax.sharding import PartitionSpec as P

MESH = pl.DeviceIdType.MESH
HI = lax.Precision.HIGHEST
F = jnp.float32
BF = jnp.bfloat16
NB = 256
SB = 128
SIDE = 4

TREE = {
    (0, 1): (1, 0), (3, 0): (-1, 0), (0, 3): (1, 0), (1, 0): (-1, 0), (0, 2): (1, 0),
    (2, 0): (-1, 0), (1, 1): (-1, 0), (3, 1): (0, 1), (3, 3): (0, -1), (1, 3): (-1, 0),
    (1, 2): (-1, 0), (2, 1): (0, 1), (3, 2): (0, -1), (2, 3): (-1, 0), (2, 2): (0, 1),
}
STEPS = ((1, 0), (-1, 0), (0, 1), (0, -1))
CHUNKS = 4


def tree_parents():
    trees = [TREE]
    for _ in range(3):
        trees.append({((-x) % SIDE, z): (-s, d) for (z, x), (d, s) in trees[-1].items()})
    return trees


def children(tree, step):
    return [
        (v[0] - step[0]) % SIDE * SIDE + (v[1] - step[1]) % SIDE
        for v, d in tree.items()
        if d == step
    ]


def one_of(value, options):
    found = value == options[0]
    for other in options[1:]:
        found = found | (value == other)
    return found


def factor_block(x, after_leaf):
    n = x.shape[0]
    leaves = n // 8
    rows = [x[8 * i : 8 * i + 8] for i in range(leaves)]
    lane = lax.broadcasted_iota(jnp.int32, (8, n), 1)
    sub = lax.broadcasted_iota(jnp.int32, (8, n), 0)
    out = []
    for b in range(leaves):
        o = 8 * b
        c = [jnp.broadcast_to(rows[b][:, o + k : o + k + 1], (8, n)) for k in range(8)]
        inside = (lane >= o) & (lane < o + 8)
        g = jnp.where(inside, jnp.where(lane - o == sub, F(1), F(0)), rows[b])
        r = jnp.zeros_like(g)
        for j in range(8):
            pivot = jnp.broadcast_to(c[j][j : j + 1], (8, n))
            inv = 1.0 / pivot
            row = jnp.broadcast_to(g[j : j + 1], (8, n))
            here = sub == j
            r = jnp.where(here, row * lax.rsqrt(pivot), r)
            grow = row * inv
            g = jnp.where(here, grow, g - c[j] * grow)
            for k in range(j + 1, 8):
                ck = jnp.broadcast_to(c[k][j : j + 1], (8, n)) * inv
                c[k] = jnp.where(here, ck, c[k] - c[j] * ck)
        out.append(r)
        if b + 1 < leaves:
            below = rows[b + 1]
            acc = jnp.where(inside, F(0), below)
            for k in range(8):
                acc = acc - jnp.broadcast_to(below[:, o + k : o + k + 1], (8, n)) * jnp.broadcast_to(
                    g[k : k + 1], (8, n)
                )
            rows[b + 1] = acc
        if b + 2 < leaves:
            rest = jnp.concatenate(rows[b + 2 :], axis=0)
            parts = [g, jnp.zeros((n - o - 8, n), F)]
            if o:
                parts = [jnp.zeros((o, n), F)] + parts
            lanes = lax.broadcasted_iota(jnp.int32, rest.shape, 1)
            cleared = jnp.where((lanes >= o) & (lanes < o + 8), F(0), rest)
            rest = cleared - jnp.dot(rest, jnp.concatenate(parts, axis=0), precision=HI, preferred_element_type=F)
            for i in range(b + 2, leaves):
                rows[i] = rest[8 * (i - b - 2) : 8 * (i - b - 2) + 8]
        after_leaf()
    return jnp.concatenate(out, axis=0)


def factor_all(d_ref, w_ref, after_leaf, after_first):
    n = w_ref.shape[0]
    li = lax.broadcasted_iota(jnp.int32, (SB, SB), 1)
    si = lax.broadcasted_iota(jnp.int32, (SB, SB), 0)
    for r0 in range(0, n, SB):
        src = w_ref if r0 else d_ref
        here = pl.ds(r0, SB)
        f = factor_block(src[here, here], after_leaf)
        if not r0:
            after_first()
        w = jnp.where(li <= si, f, F(0))
        w_ref[here, :] = jnp.dot(w, src[here, :], precision=HI, preferred_element_type=F)
        w_ref[here, here] = w
        k0 = r0 + SB
        if k0 < n:
            rr = w_ref[here, :]
            upd = lax.dot_general(
                rr[:, k0:], rr, (((0,), (0,)), ((), ())), precision=HI, preferred_element_type=F
            )
            col = lax.broadcasted_iota(jnp.int32, (n - k0, n), 1)
            old = jnp.where((col >= r0) & (col < k0), F(0), src[pl.ds(k0, n - k0), :])
            w_ref[pl.ds(k0, n - k0), :] = old - upd
            w_ref[here, pl.ds(k0, n - k0)] = jnp.zeros((SB, n - k0), F)


def gather_kernel(x_ref, a_ref, t_ref, r_ref, w_ref, d_ref, sem_local, sem_stage, t_send, t_recv, r_send, r_recv, d_send, d_recv):
    p = lax.axis_index("prow")
    q = lax.axis_index("pcol")
    z, x = p // SIDE, p % SIDE
    y, c = q // 2, q % 2
    tiles = x_ref.shape[3]
    row_tiles = x_ref.shape[0]

    def dev(dz=0, dx=0, dy=0, other=False):
        cc = 1 - c if other else c
        return {
            "prow": (z + dz + SIDE) % SIDE * SIDE + (x + dx + SIDE) % SIDE,
            "pcol": (y + dy + SIDE) % SIDE * 2 + cc,
        }

    stage = []
    for k in range(2):
        for j in range(tiles):
            stage.append(
                (
                    p == k,
                    pltpu.make_async_copy(
                        x_ref.at[0, 0, :, j, 0, :],
                        t_ref.at[pl.ds(NB * k, NB), pl.ds(NB * j, NB)],
                        sem_stage.at[len(stage)],
                    ),
                )
            )
    for row, col in ((0, 0), (0, 1), (1, 1)):
        stage.append(
            (
                (p == row) & (q == col),
                pltpu.make_async_copy(
                    x_ref.at[0, 0, :, 0, 0, :],
                    d_ref.at[pl.ds(NB * row, NB), pl.ds(NB * col, NB)],
                    sem_stage.at[len(stage)],
                ),
            )
        )
    for k in range(2):
        for i in range(row_tiles):
            stage.append(
                (
                    q == k,
                    pltpu.make_async_copy(
                        x_ref.at[i, 0, :, 0, 0, :], r_ref.at[k, pl.ds(NB * i, NB), :], sem_stage.at[len(stage)]
                    ),
                )
            )
    for cond, copy in stage:
        pl.when(cond)(copy.start)
    own = [
        pltpu.make_async_copy(
            x_ref.at[i, 0, :, j, 0, :],
            a_ref.at[pl.ds(NB * i, NB), pl.ds(NB * j, NB)],
            sem_local.at[i * tiles + j],
        )
        for i in range(row_tiles)
        for j in range(tiles)
    ]
    for copy in own:
        copy.start()

    barrier = pltpu.get_barrier_semaphore()
    peers = [dev(other=True)]
    for s in range(1, SIDE):
        peers += [dev(dz=s), dev(dx=s), dev(dy=s)]
    for peer in peers:
        pl.semaphore_signal(barrier, inc=1, device_id=peer, device_id_type=MESH)
    pl.semaphore_wait(barrier, len(peers))
    for cond, copy in stage:
        pl.when(cond)(copy.wait)

    sends = []

    def remote(ref, send, recv, peer):
        return pltpu.make_async_remote_copy(
            src_ref=ref, dst_ref=ref, send_sem=send, recv_sem=recv, device_id=peer, device_id_type=MESH
        )

    def send(cond, copy):
        pl.when(cond)(copy.start)
        sends.append((cond, copy))

    def line(s):
        return ((s == 0, 1), (s == 0, 3), (s == 1, 1))

    pieces = [
        (0, 128, 0, 128, 0, 0),
        (0, 256, 128, 256, 0, 0),
        (0, 256, 256, 512, 0, 1),
        (256, 512, 256, 512, 1, 1),
    ]

    def lead_piece(i):
        ra, rb, ca, cb, x0, c0 = pieces[i]
        ref = d_ref.at[pl.ds(ra, rb - ra), pl.ds(ca, cb - ca)]
        mine = c == c0
        root = mine & (z == 0) & (x == x0) & (y == 0)
        rx = (x - x0 + SIDE) % SIDE

        @pl.when(jnp.logical_not(root))
        def _():
            remote(ref, d_send.at[i, 0], d_recv.at[i], dev(other=True)).wait_recv()

        for j, (cond, step) in enumerate(line(y)):
            send(mine & (z == 0) & (rx == 0) & cond, remote(ref, d_send.at[i, j], d_recv.at[i], dev(dy=step)))
        for j, (cond, step) in enumerate(line(z)):
            send(mine & (rx == 0) & cond, remote(ref, d_send.at[i, 3 + j], d_recv.at[i], dev(dz=step)))
        for j, (cond, step) in enumerate(line(rx)):
            send(mine & cond, remote(ref, d_send.at[i, 6 + j], d_recv.at[i], dev(dx=step)))
        send(mine, remote(ref, d_send.at[i, 9], d_recv.at[i], dev(other=True)))

    def row_chain(i):
        down = i >= row_tiles // 2
        step = SIDE - 1 if down else 1
        for k in range(2):
            ref = r_ref.at[k, pl.ds(NB * i, NB), :]
            mine = c == k
            last = 1 if down else SIDE - 1

            @pl.when(mine & (y != 0))
            def _():
                remote(ref, r_send.at[k, i, 0], r_recv.at[k, i], dev(dy=step)).wait_recv()

            send(mine & (y != last), remote(ref, r_send.at[k, i, 0], r_recv.at[k, i], dev(dy=step)))
            send(mine, remote(ref, r_send.at[k, i, 1], r_recv.at[k, i], dev(other=True)))

    def row_partner(i):
        for k in range(2):
            ref = r_ref.at[k, pl.ds(NB * i, NB), :]

            @pl.when(c != k)
            def _():
                remote(ref, r_send.at[k, i, 1], r_recv.at[k, i], dev(other=True)).wait_recv()

    trees = tree_parents()
    rel = [z * SIDE + (x - k + SIDE) % SIDE for k in range(2)]
    has = [[[one_of(rel[k], children(t, s)) for s in STEPS] for t in trees] for k in range(2)]
    share = NB // len(trees)
    size = share // CHUNKS

    def tree_chunk(k, t, i):
        e = (k * len(trees) + t) * CHUNKS + i
        ref = t_ref.at[pl.ds(NB * k + share * t + size * i, size), :]

        @pl.when(rel[k] != 0)
        def _():
            remote(ref, t_send.at[e, 0], t_recv.at[e], dev(other=True)).wait_recv()

        for j, (dz, dx) in enumerate(STEPS):
            send(has[k][t][j], remote(ref, t_send.at[e, j], t_recv.at[e], dev(dz=dz, dx=dx)))

    todo = [functools.partial(lead_piece, i) for i in range(1, len(pieces))]
    trees_todo = [
        functools.partial(tree_chunk, k, t, i)
        for i in range(CHUNKS)
        for k in range(2)
        for t in range(len(trees))
    ]
    order = [row_tiles // 2, 0, row_tiles // 2 + 1, 1]
    chains = [functools.partial(row_chain, i) for i in order]
    partners = [functools.partial(row_partner, i) for i in order]
    queue = []
    for n, item in enumerate(trees_todo):
        queue.append(item)
        if n % 2 == 1 and chains:
            queue.append(chains.pop(0))
        elif n >= 12 and n % 2 == 1 and partners:
            queue.append(partners.pop(0))

    def after_leaf():
        for _ in range(1 if todo else 2):
            if todo:
                todo.pop(0)()
            elif queue:
                queue.pop(0)()

    lead_piece(0)

    def after_first():
        while todo:
            todo.pop(0)()

    factor_all(d_ref, w_ref, after_leaf, after_first)
    while queue:
        queue.pop(0)()
    for cond, copy in sends:
        pl.when(cond)(copy.wait_send)
    for copy in own:
        copy.wait()


def split(v):
    hi = v.astype(BF)
    return hi, (v - hi.astype(F)).astype(BF)


def dot(a, b):
    return jnp.dot(a, b, preferred_element_type=F)


def update_kernel(a_ref, t_ref, r_ref, w_ref, o_ref, thi, tlo, buf, sem):
    p = lax.axis_index("prow")
    q = lax.axis_index("pcol")
    prows = lax.axis_size("prow")
    tiles = a_ref.shape[1] // NB
    row_tiles = a_ref.shape[0] // NB
    ri = lax.broadcasted_iota(jnp.int32, (NB, NB), 0)
    ci = lax.broadcasted_iota(jnp.int32, (NB, NB), 1)
    for j in range(tiles):
        sl = pl.ds(NB * j, NB)
        hi, lo = split(t_ref[:, sl])
        thi[:, sl] = hi
        tlo[:, sl] = lo

    def copies(i, j):
        return pltpu.make_async_copy(
            buf.at[i % 2, :, pl.ds(NB * j, NB)], o_ref.at[i, 0, :, j, 0, :], sem.at[i % 2, j]
        )

    def body(i, carry):
        rows = pl.ds(pl.multiple_of(i * NB, NB), NB)
        ar = jnp.concatenate([r_ref[0, rows, :], r_ref[1, rows, :]], axis=1)
        w = w_ref[...]
        pr = lax.dot_general(ar, w, (((1,), (1,)), ((), ())), precision=HI, preferred_element_type=F)
        bhi, blo = split(jnp.dot(pr, w, precision=HI, preferred_element_type=F))
        row = i * prows + p
        active = row > 1

        @pl.when(i >= 2)
        def _():
            for j in range(tiles):
                copies(i - 2, j).wait()

        for j in range(tiles):
            sl = pl.ds(NB * j, NB)
            hi, lo = thi[:, sl], tlo[:, sl]
            val = a_ref[rows, sl] - (dot(bhi, hi) + (dot(bhi, lo) + dot(blo, hi)))
            val = jnp.where(active, val, F(0))
            if j == 0:
                panel = jnp.where(q == 0, pr[:, :NB], pr[:, NB:])
                keep = (row > q) | ((row == q) & (ci <= ri))
                val = jnp.where(q < 2, jnp.where(keep, panel, F(0)), val)
            buf[i % 2, :, sl] = val
            copies(i, j).start()
        return carry

    lax.fori_loop(0, row_tiles, body, 0)
    for i in range(row_tiles - 2, row_tiles):
        for j in range(tiles):
            copies(i, j).wait()


def shards(kernel_tiles):
    row_tiles, _, nb, tiles, _, _ = kernel_tiles.shape
    rows, cols, lead = row_tiles * nb, tiles * nb, 2 * nb
    vmem = pl.BlockSpec(memory_space=pltpu.VMEM)
    dma = pltpu.SemaphoreType.DMA
    events = 2 * 4 * CHUNKS
    a, t, r, w = pl.pallas_call(
        gather_kernel,
        out_shape=[
            jax.ShapeDtypeStruct((rows, cols), F),
            jax.ShapeDtypeStruct((lead, cols), F),
            jax.ShapeDtypeStruct((2, rows, nb), F),
            jax.ShapeDtypeStruct((lead, lead), F),
        ],
        in_specs=[pl.BlockSpec(memory_space=pltpu.HBM)],
        out_specs=[vmem] * 4,
        scratch_shapes=[
            pltpu.VMEM((lead, lead), F),
            dma((row_tiles * tiles,)),
            dma((2 * tiles + 3 + 2 * row_tiles,)),
            dma((events, 4)),
            dma((events,)),
            dma((2, row_tiles, 2)),
            dma((2, row_tiles)),
            dma((4, 10)),
            dma((4,)),
        ],
        compiler_params=pltpu.CompilerParams(
            collective_id=0, has_side_effects=True, vmem_limit_bytes=24 * 2**20
        ),
        name="gather_and_factor",
    )(kernel_tiles)
    return pl.pallas_call(
        update_kernel,
        out_shape=jax.ShapeDtypeStruct(kernel_tiles.shape, F),
        in_specs=[vmem] * 4,
        out_specs=pl.BlockSpec(memory_space=pl.ANY),
        scratch_shapes=[
            pltpu.VMEM((lead, cols), BF),
            pltpu.VMEM((lead, cols), BF),
            pltpu.VMEM((2, nb, cols), F),
            dma((2, tiles)),
        ],
        compiler_params=pltpu.CompilerParams(vmem_limit_bytes=28 * 2**20),
        name="update",
    )(a, t, r, w)


def solution(mesh):
    spec = P(None, "prow", None, None, "pcol", None)
    return jax.shard_map(shards, mesh=mesh, in_specs=(spec,), out_specs=spec, check_vma=False)
```

time: 621 us -> 420 us (0.68); the launches traced: 609 us -> 420 us
  Pallas kernels: 0 us -> 417 us
  waiting for transfers between devices: 379 us -> 0 us
  other arithmetic: 125 us -> 0 us
  local copies, waits for them, and re-layouts: 58.9 us -> 3.38 us
  matrix products: 28.1 us -> 0 us
  between operations: 16.5 us -> 0.21 us
    pallas_call x0 -> x2, Pallas kernels: none -> 417 us  [the longest x1 389 us: shards(): pl.pallas_call(gather_kernel, out_shape=[jax.ShapeDtypeStruct((rows, cols...]
    all_gather x4 -> x0, waiting for transfers between devices: 197 us -> none  [picked(): lax.all_gather(shard, axis)]
    psum x2 -> x0, waiting for transfers between devices: 182 us -> none  [from_root(): return lax.psum(jnp.where(mine, shard, jnp.zeros_like(shard)), axis)]
    another operation x20 -> x0, other arithmetic: 117 us -> none  [the longest x13 68.6 us: factor_panel(): factor = jnp.linalg.cholesky(local_block[tile_row, :, tile_col, :])]
    dot_general x2 -> x0, matrix products: 23.5 us -> none  [trailing(): jnp.einsum('arn,csn->arcs', row_panel, col_panel, precision=highest)]
    reshape x2 -> x0, local copies, waits for them, and re-layouts: 20.9 us -> none  [the longest x1 20.5 us: shards(): return result.reshape(kernel_tiles.shape)]
    unnamed x3 -> x2, local copies, waits for them, and re-layouts: 23.9 us -> 3.38 us
    another operation x23 -> x0, local copies, waits for them, and re-layouts: 8.58 us -> none  [the longest x15 7.59 us: tile_solve(): solved = jax.scipy.linalg.solve_triangular(factor, flat_rows.T, lower=True)]
  transfers between devices with their start and end apart: 6 -> 0, of which waited for: 6 -> 0; matrix products, arithmetic and copies ran while one was open for 1% -> 0% of each run, Pallas kernels for 0% -> 0%
where the time goes in v1:
time: 420 us
  Pallas kernels  417 us (99%)
    pallas_call x1, Pallas kernels, shards(): pl.pallas_call(gather_kernel, out_shape=[jax.ShapeDtypeStruct((rows, cols...  389 us
    pallas_call x1, Pallas kernels, shards(): pl.pallas_call(update_kernel, out_shape=jax.ShapeDtypeStruct(kernel_tiles...  27.9 us

profile of v1, /device:TPU:88, one launch (start us, length us, event | category | flops | bytes accessed | tf_op | source)
XLA Modules:
  0.0 420.3 jit_solution(10181717935428128864)
XLA Ops:
  0.0 0.0 copy-start
  0.0 3.4 copy-done
  3.4 388.8 %gather_and_factor.1 = (f32[1024,2048]{1,0:T(8,128)S(1)}, f32[512,2048]{1,0:T(8,128)S(1)}, f32[2,1024,256]{2,1,0:T(8,128)S(1)}, f32[512,512]{1,0:T(8,128)S(1)}) custom-call(f32[4,1,256,8,1,256]{5,4,3,2,1,0:T(1,128)S(1)} %copy-done), custom_call_target="tpu_custom_call" | custom-call | tf_op jit(solution)/shard_map/gather_and_factor/pallas_call | solution.py:381
  392.2 27.9 %update.1 = f32[4,1,256,8,1,256]{5,4,3,2,1,0:T(1,128)} custom-call(f32[1024,2048]{1,0:T(8,128)S(1)} %get-tuple-element.9.a_ref, f32[512,2048]{1,0:T(8,128)S(1)} %get-tuple-element.10.t_ref, f32[2,1024,256]{2,1,0:T(8,128)S(1)} %get-tuple-element.11.r_ref, f32[512,512]{1,0:T(8,128)S(1)} %get-tuple-element.12.w_ref), custom_call_target="tpu_custom_call" | custom-call | tf_op jit(solution)/shard_map/update/pallas_call | solution.py:407
Async XLA Ops:
  0.0 3.4 copy-start

commit v2 on v1

--- a/solution.py
+++ b/solution.py
@@ -21,7 +21,7 @@
     (1, 2): (-1, 0), (2, 1): (0, 1), (3, 2): (0, -1), (2, 3): (-1, 0), (2, 2): (0, 1),
 }
 STEPS = ((1, 0), (-1, 0), (0, 1), (0, -1))
-CHUNKS = 4
+LAG = 2
 
 
 def tree_parents():
@@ -37,6 +37,17 @@
         for v, d in tree.items()
         if d == step
     ]
+
+
+def depths(tree):
+    def depth(v):
+        if v == (0, 0):
+            return 0
+        z, x = v
+        d, s = tree[v]
+        return 1 + depth(((z - d) % SIDE, (x - s) % SIDE))
+
+    return [depth((v // SIDE, v % SIDE)) for v in range(SIDE * SIDE)]
 
 
 def one_of(value, options):
@@ -118,13 +129,17 @@
             w_ref[here, pl.ds(k0, n - k0)] = jnp.zeros((SB, n - k0), F)
 
 
-def gather_kernel(x_ref, a_ref, t_ref, r_ref, w_ref, d_ref, sem_local, sem_stage, t_send, t_recv, r_send, r_recv, d_send, d_recv):
+def gather_kernel(
+    x_ref, a_ref, t_ref, r_ref, w_ref, d_ref,
+    sem_local, sem_stage, t_send, t_recv, top_send, top_recv, u_send, u_recv, r_send, r_recv, d_send, d_recv, w_send, w_recv,
+):
     p = lax.axis_index("prow")
     q = lax.axis_index("pcol")
     z, x = p // SIDE, p % SIDE
     y, c = q // 2, q % 2
     tiles = x_ref.shape[3]
     row_tiles = x_ref.shape[0]
+    first, second = c == 0, c == 1
 
     def dev(dz=0, dx=0, dy=0, other=False):
         cc = 1 - c if other else c
@@ -133,40 +148,30 @@
             "pcol": (y + dy + SIDE) % SIDE * 2 + cc,
         }
 
+    partner = dev(other=True)
+
     stage = []
+
+    def bring(cond, src, dst):
+        stage.append((cond, pltpu.make_async_copy(src, dst, sem_stage.at[len(stage)])))
+
+    for row, col in ((0, 0), (0, 1), (1, 1)):
+        bring(
+            (p == row) & (q == col),
+            x_ref.at[0, 0, :, 0, 0, :],
+            d_ref.at[pl.ds(NB * row, NB), pl.ds(NB * col, NB)],
+        )
     for k in range(2):
         for j in range(tiles):
-            stage.append(
-                (
-                    p == k,
-                    pltpu.make_async_copy(
-                        x_ref.at[0, 0, :, j, 0, :],
-                        t_ref.at[pl.ds(NB * k, NB), pl.ds(NB * j, NB)],
-                        sem_stage.at[len(stage)],
-                    ),
+            for slot in range(2):
+                bring(
+                    (p == k) & (c == slot),
+                    x_ref.at[0, 0, :, j, 0, :],
+                    t_ref.at[slot, pl.ds(NB * k, NB), pl.ds(NB * j, NB)],
                 )
-            )
-    for row, col in ((0, 0), (0, 1), (1, 1)):
-        stage.append(
-            (
-                (p == row) & (q == col),
-                pltpu.make_async_copy(
-                    x_ref.at[0, 0, :, 0, 0, :],
-                    d_ref.at[pl.ds(NB * row, NB), pl.ds(NB * col, NB)],
-                    sem_stage.at[len(stage)],
-                ),
-            )
-        )
     for k in range(2):
         for i in range(row_tiles):
-            stage.append(
-                (
-                    q == k,
-                    pltpu.make_async_copy(
-                        x_ref.at[i, 0, :, 0, 0, :], r_ref.at[k, pl.ds(NB * i, NB), :], sem_stage.at[len(stage)]
-                    ),
-                )
-            )
+            bring(q == k, x_ref.at[i, 0, :, 0, 0, :], r_ref.at[k, pl.ds(NB * i, NB), :])
     for cond, copy in stage:
         pl.when(cond)(copy.start)
     own = [
@@ -182,7 +187,7 @@
         copy.start()
 
     barrier = pltpu.get_barrier_semaphore()
-    peers = [dev(other=True)]
+    peers = [partner]
     for s in range(1, SIDE):
         peers += [dev(dz=s), dev(dx=s), dev(dy=s)]
     for peer in peers:
@@ -193,17 +198,14 @@
 
     sends = []
 
-    def remote(ref, send, recv, peer):
+    def remote(src, dst, send, recv, peer):
         return pltpu.make_async_remote_copy(
-            src_ref=ref, dst_ref=ref, send_sem=send, recv_sem=recv, device_id=peer, device_id_type=MESH
+            src_ref=src, dst_ref=dst, send_sem=send, recv_sem=recv, device_id=peer, device_id_type=MESH
         )
 
     def send(cond, copy):
         pl.when(cond)(copy.start)
         sends.append((cond, copy))
-
-    def line(s):
-        return ((s == 0, 1), (s == 0, 3), (s == 1, 1))
 
     pieces = [
         (0, 128, 0, 128, 0, 0),
@@ -212,39 +214,49 @@
         (256, 512, 256, 512, 1, 1),
     ]
 
+    def line(s, direct):
+        return ((s == 0, 1), (s == 0, 3), (s == 0 if direct else s == 1, 2 if direct else 1))
+
+    def piece_ref(i):
+        ra, rb, ca, cb, _, _ = pieces[i]
+        return d_ref.at[pl.ds(ra, rb - ra), pl.ds(ca, cb - ca)]
+
+    def hand_over(i):
+        root = first & (z == 0) & (x == pieces[i][4]) & (y == 0)
+        ref = piece_ref(i)
+        send(root, remote(ref, ref, d_send.at[i, 9], d_recv.at[i], partner))
+
     def lead_piece(i):
-        ra, rb, ca, cb, x0, c0 = pieces[i]
-        ref = d_ref.at[pl.ds(ra, rb - ra), pl.ds(ca, cb - ca)]
-        mine = c == c0
-        root = mine & (z == 0) & (x == x0) & (y == 0)
+        x0, c0 = pieces[i][4:]
+        ref = piece_ref(i)
         rx = (x - x0 + SIDE) % SIDE
-
-        @pl.when(jnp.logical_not(root))
+        source = second & (z == 0) & (rx == 0) & (y == 0)
+
+        @pl.when(second if c0 == 0 else second & jnp.logical_not(source))
         def _():
-            remote(ref, d_send.at[i, 0], d_recv.at[i], dev(other=True)).wait_recv()
-
-        for j, (cond, step) in enumerate(line(y)):
-            send(mine & (z == 0) & (rx == 0) & cond, remote(ref, d_send.at[i, j], d_recv.at[i], dev(dy=step)))
-        for j, (cond, step) in enumerate(line(z)):
-            send(mine & (rx == 0) & cond, remote(ref, d_send.at[i, 3 + j], d_recv.at[i], dev(dz=step)))
-        for j, (cond, step) in enumerate(line(rx)):
-            send(mine & cond, remote(ref, d_send.at[i, 6 + j], d_recv.at[i], dev(dx=step)))
-        send(mine, remote(ref, d_send.at[i, 9], d_recv.at[i], dev(other=True)))
-
-    def row_chain(i):
+            remote(ref, ref, d_send.at[i, 0], d_recv.at[i], partner).wait_recv()
+
+        direct = i == 0
+        for j, (cond, step) in enumerate(line(y, direct)):
+            send(second & (z == 0) & (rx == 0) & cond, remote(ref, ref, d_send.at[i, j], d_recv.at[i], dev(dy=step)))
+        for j, (cond, step) in enumerate(line(z, direct)):
+            send(second & (rx == 0) & cond, remote(ref, ref, d_send.at[i, 3 + j], d_recv.at[i], dev(dz=step)))
+        for j, (cond, step) in enumerate(line(rx, direct)):
+            send(second & cond, remote(ref, ref, d_send.at[i, 6 + j], d_recv.at[i], dev(dx=step)))
+
+    def row_chain(k, i):
         down = i >= row_tiles // 2
         step = SIDE - 1 if down else 1
-        for k in range(2):
-            ref = r_ref.at[k, pl.ds(NB * i, NB), :]
-            mine = c == k
-            last = 1 if down else SIDE - 1
-
-            @pl.when(mine & (y != 0))
-            def _():
-                remote(ref, r_send.at[k, i, 0], r_recv.at[k, i], dev(dy=step)).wait_recv()
-
-            send(mine & (y != last), remote(ref, r_send.at[k, i, 0], r_recv.at[k, i], dev(dy=step)))
-            send(mine, remote(ref, r_send.at[k, i, 1], r_recv.at[k, i], dev(other=True)))
+        ref = r_ref.at[k, pl.ds(NB * i, NB), :]
+        mine = c == k
+        last = 1 if down else SIDE - 1
+
+        @pl.when(mine & (y != 0))
+        def _():
+            remote(ref, ref, r_send.at[k, i, 0], r_recv.at[k, i], dev(dy=step)).wait_recv()
+
+        send(mine & (y != last), remote(ref, ref, r_send.at[k, i, 0], r_recv.at[k, i], dev(dy=step)))
+        send(mine, remote(ref, ref, r_send.at[k, i, 1], r_recv.at[k, i], partner))
 
     def row_partner(i):
         for k in range(2):
@@ -252,59 +264,131 @@
 
             @pl.when(c != k)
             def _():
-                remote(ref, r_send.at[k, i, 1], r_recv.at[k, i], dev(other=True)).wait_recv()
+                remote(ref, ref, r_send.at[k, i, 1], r_recv.at[k, i], partner).wait_recv()
+
+    order = [row_tiles // 2, 0, row_tiles // 2 + 1, 1]
 
     trees = tree_parents()
     rel = [z * SIDE + (x - k + SIDE) % SIDE for k in range(2)]
     has = [[[one_of(rel[k], children(t, s)) for s in STEPS] for t in trees] for k in range(2)]
+    deep = [depths(t) for t in trees]
+    depth = [
+        [sum(jnp.where(rel[k] == v, d, 0) for v, d in enumerate(deep[t])) for t in range(len(trees))]
+        for k in range(2)
+    ]
+    most = max(max(d) for d in deep)
     share = NB // len(trees)
-    size = share // CHUNKS
-
-    def tree_chunk(k, t, i):
-        e = (k * len(trees) + t) * CHUNKS + i
-        ref = t_ref.at[pl.ds(NB * k + share * t + size * i, size), :]
-
-        @pl.when(rel[k] != 0)
+    count = share // 8 * 2
+    peer4 = [dev(dz=dz, dx=dx) for dz, dx in STEPS]
+
+    def chunk(k, t, i):
+        start = pl.multiple_of(NB * k + share * t + i // 2 * 8, 8)
+        return lambda slot: t_ref.at[slot, pl.ds(start, 8), :]
+
+    def hop(k, t, i, j):
+        e = k * len(trees) + t
+        ref = chunk(k, t, i)(i % 2)
+        return remote(ref, ref, t_send.at[e, i, j], t_recv.at[e, i], peer4[j])
+
+    def over(k, t, i):
+        e = k * len(trees) + t
+        ref = chunk(k, t, i)
+        return remote(ref(1), ref(0), u_send.at[e, i], u_recv.at[e], partner)
+
+    def each(s, action):
+        for k in range(2):
+            for t in range(len(trees)):
+                i = s - LAG * depth[k][t]
+
+                @pl.when((i >= 0) & (i < count))
+                def _():
+                    action(k, t, i)
+
+    def forward(k, t, i):
+        @pl.when(depth[k][t] != 0)
         def _():
-            remote(ref, t_send.at[e, 0], t_recv.at[e], dev(other=True)).wait_recv()
-
-        for j, (dz, dx) in enumerate(STEPS):
-            send(has[k][t][j], remote(ref, t_send.at[e, j], t_recv.at[e], dev(dz=dz, dx=dx)))
+            hop(k, t, i, 0).wait_recv()
+
+        for j in range(len(STEPS)):
+            pl.when(has[k][t][j])(hop(k, t, i, j).start)
+        pl.when(i % 2 == 1)(over(k, t, i).start)
+
+    def sent(k, t, i):
+        for j in range(len(STEPS)):
+            pl.when(has[k][t][j])(hop(k, t, i, j).wait_send)
+        pl.when(i % 2 == 1)(over(k, t, i).wait_send)
+
+    steps = count + LAG * most
+
+    def wave(lo, hi):
+        def body(s, carry):
+            each(s, forward)
+            each(s - 8, sent)
+            return carry
+
+        lax.fori_loop(lo, hi, body, 0)
+
+    tops = [
+        remote(t_ref.at[1, pl.ds(NB * k, NB), :], t_ref.at[1, pl.ds(NB * k, NB), :], top_send.at[k], top_recv.at[k], partner)
+        for k in range(2)
+    ]
+    for i in range(2):
+        hand_over(i)
+    for k in range(2):
+        send(second & (p == k), tops[k])
+
+    for i in range(len(pieces) if False else 1):
+        lead_piece(i)
 
     todo = [functools.partial(lead_piece, i) for i in range(1, len(pieces))]
-    trees_todo = [
-        functools.partial(tree_chunk, k, t, i)
-        for i in range(CHUNKS)
-        for k in range(2)
-        for t in range(len(trees))
-    ]
-    order = [row_tiles // 2, 0, row_tiles // 2 + 1, 1]
-    chains = [functools.partial(row_chain, i) for i in order]
-    partners = [functools.partial(row_partner, i) for i in order]
-    queue = []
-    for n, item in enumerate(trees_todo):
-        queue.append(item)
-        if n % 2 == 1 and chains:
-            queue.append(chains.pop(0))
-        elif n >= 12 and n % 2 == 1 and partners:
-            queue.append(partners.pop(0))
+    todo += [functools.partial(row_chain, 1, i) for i in order]
 
     def after_leaf():
-        for _ in range(1 if todo else 2):
-            if todo:
-                todo.pop(0)()
-            elif queue:
-                queue.pop(0)()
-
-    lead_piece(0)
-
-    def after_first():
-        while todo:
+        if todo:
             todo.pop(0)()
 
-    factor_all(d_ref, w_ref, after_leaf, after_first)
-    while queue:
-        queue.pop(0)()
+    @pl.when(first)
+    def _():
+        for k in range(2):
+            pl.when(p == k)(tops[k].wait_recv)
+        wave(0, 4)
+
+    row_chain(0, order[0])
+    row_chain(0, order[1])
+
+    @pl.when(first)
+    def _():
+        wave(4, 8)
+
+    row_chain(0, order[2])
+    row_chain(0, order[3])
+
+    @pl.when(first)
+    def _():
+        wave(8, steps + 8)
+
+    for item in todo:
+        item()
+
+    @pl.when(second)
+    def _():
+        factor_all(d_ref, w_ref, lambda: None, lambda: None)
+
+    send(second, remote(w_ref, w_ref, w_send.at[0], w_recv.at[0], partner))
+
+    @pl.when(first)
+    def _():
+        remote(w_ref, w_ref, w_send.at[0], w_recv.at[0], partner).wait_recv()
+
+    @pl.when(second)
+    def _():
+        for k in range(2):
+            for t in range(len(trees)):
+                ref = t_ref.at[0, pl.ds(NB * k + share * t, share), :]
+                remote(ref, ref, u_send.at[0, 0], u_recv.at[k * len(trees) + t], partner).wait_recv()
+
+    for i in order:
+        row_partner(i)
     for cond, copy in sends:
         pl.when(cond)(copy.wait_send)
     for copy in own:
@@ -330,7 +414,7 @@
     ci = lax.broadcasted_iota(jnp.int32, (NB, NB), 1)
     for j in range(tiles):
         sl = pl.ds(NB * j, NB)
-        hi, lo = split(t_ref[:, sl])
+        hi, lo = split(t_ref[0, :, sl])
         thi[:, sl] = hi
         tlo[:, sl] = lo
 
@@ -377,12 +461,12 @@
     rows, cols, lead = row_tiles * nb, tiles * nb, 2 * nb
     vmem = pl.BlockSpec(memory_space=pltpu.VMEM)
     dma = pltpu.SemaphoreType.DMA
-    events = 2 * 4 * CHUNKS
+    count = nb // 4 // 8 * 2
     a, t, r, w = pl.pallas_call(
         gather_kernel,
         out_shape=[
             jax.ShapeDtypeStruct((rows, cols), F),
-            jax.ShapeDtypeStruct((lead, cols), F),
+            jax.ShapeDtypeStruct((2, lead, cols), F),
             jax.ShapeDtypeStruct((2, rows, nb), F),
             jax.ShapeDtypeStruct((lead, lead), F),
         ],
@@ -391,16 +475,22 @@
         scratch_shapes=[
             pltpu.VMEM((lead, lead), F),
             dma((row_tiles * tiles,)),
-            dma((2 * tiles + 3 + 2 * row_tiles,)),
-            dma((events, 4)),
-            dma((events,)),
+            dma((4 * tiles + 3 + 2 * row_tiles,)),
+            dma((8, count, 4)),
+            dma((8, count)),
+            dma((2,)),
+            dma((2,)),
+            dma((8, count)),
+            dma((8,)),
             dma((2, row_tiles, 2)),
             dma((2, row_tiles)),
             dma((4, 10)),
             dma((4,)),
+            dma((1,)),
+            dma((1,)),
         ],
         compiler_params=pltpu.CompilerParams(
-            collective_id=0, has_side_effects=True, vmem_limit_bytes=24 * 2**20
+            collective_id=0, has_side_effects=True, vmem_limit_bytes=44 * 2**20
         ),
         name="gather_and_factor",
     )(kernel_tiles)

time: 420 us -> 159 us (0.38)
  Pallas kernels: 417 us -> 150 us
    pallas_call x1, Pallas kernels: 389 us -> 123 us  [shards(): pl.pallas_call(gather_kernel, out_shape=[jax.ShapeDtypeStruct((rows, cols...]
where the time goes in v2:
time: 159 us; the launch traced here: 157 us
  Pallas kernels  150 us (94%)
  local copies, waits for them, and re-layouts  6.76 us (4%)
    pallas_call x1, Pallas kernels, shards(): pl.pallas_call(gather_kernel, out_shape=[jax.ShapeDtypeStruct((rows, cols...  123 us
    pallas_call x1, Pallas kernels, shards(): pl.pallas_call(update_kernel, out_shape=jax.ShapeDtypeStruct(kernel_tiles...  27.6 us
    unnamed x4, local copies, waits for them, and re-layouts  6.76 us

profile of v2, /device:TPU:88, one launch (start us, length us, event | category | flops | bytes accessed | tf_op | source)
XLA Modules:
  0.0 157.4 jit_solution(9346007799635679777)
XLA Ops:
  0.0 122.8 %gather_and_factor.1 = (f32[1024,2048]{1,0:T(8,128)}, f32[2,512,2048]{2,1,0:T(8,128)}, f32[2,1024,256]{2,1,0:T(8,128)S(1)}, f32[512,512]{1,0:T(8,128)S(1)}) custom-call(f32[4,1,256,8,1,256]{5,4,3,2,1,0:T(1,128)} %x_ref.1), custom_call_target="tpu_custom_call" | custom-call | tf_op jit(solution)/shard_map/gather_and_factor/pallas_call | solution.py:465
  122.8 0.0 copy-start
  122.8 3.4 %copy-done = f32[1024,2048]{1,0:T(8,128)S(1)} copy-done((f32[1024,2048]{1,0:T(8,128)S(1)}, f32[1024,2048]{1,0:T(8,128)}, u32[]{:S(2)}) %copy-start) | copy-done | bytes 8388632
  126.2 0.0 copy-start.1
  126.2 3.4 %copy-done.1 = f32[2,512,2048]{2,1,0:T(8,128)S(1)} copy-done((f32[2,512,2048]{2,1,0:T(8,128)S(1)}, f32[2,512,2048]{2,1,0:T(8,128)}, u32[]{:S(2)}) %copy-start.1) | copy-done | bytes 8388632
  129.6 27.6 %update.1 = f32[4,1,256,8,1,256]{5,4,3,2,1,0:T(1,128)} custom-call(f32[1024,2048]{1,0:T(8,128)S(1)} %copy-done, f32[2,512,2048]{2,1,0:T(8,128)S(1)} %copy-done.1, f32[2,1024,256]{2,1,0:T(8,128)S(1)} %get-tuple-element.11.r_ref, f32[512,512]{1,0:T(8,128)S(1)} %get-tuple-element.12.w_ref), custom_call_target="tpu_custom_call" | custom-call | tf_op jit(solution)/shard_map/update/pallas_call | solution.py:497
Async XLA Ops:
  122.8 3.4 %copy-start = (f32[1024,2048]{1,0:T(8,128)S(1)}, f32[1024,2048]{1,0:T(8,128)}, u32[]{:S(2)}) copy-start(f32[1024,2048]{1,0:T(8,128)} %get-tuple-element.9.a_ref) | copy-start | bytes 25165828
  126.2 3.4 %copy-start.1 = (f32[2,512,2048]{2,1,0:T(8,128)S(1)}, f32[2,512,2048]{2,1,0:T(8,128)}, u32[]{:S(2)}) copy-start(f32[2,512,2048]{2,1,0:T(8,128)} %get-tuple-element.10.t_ref) | copy-start | bytes 25165828

commit v3 on v2

v3 whole, which is shorter than its diff:
```python
import functools

import jax
import jax.numpy as jnp
from jax import lax
from jax.experimental import pallas as pl
from jax.experimental.pallas import tpu as pltpu
from jax.sharding import PartitionSpec as P

MESH = pl.DeviceIdType.MESH
HI = lax.Precision.HIGHEST
F = jnp.float32
BF = jnp.bfloat16
NB = 256
SB = 128
SIDE = 4

TREE = {
    (0, 1): (1, 0), (3, 0): (-1, 0), (0, 3): (1, 0), (1, 0): (-1, 0), (0, 2): (1, 0),
    (2, 0): (-1, 0), (1, 1): (-1, 0), (3, 1): (0, 1), (3, 3): (0, -1), (1, 3): (-1, 0),
    (1, 2): (-1, 0), (2, 1): (0, 1), (3, 2): (0, -1), (2, 3): (-1, 0), (2, 2): (0, 1),
}
STEPS = ((1, 0), (-1, 0), (0, 1), (0, -1))
LAG = 3
LAG_LEAD = 3
LEAD = 7
ROW_CHUNKS = 4
ROW_START = 2
EVERY = 1
SPLIT = 1
PACE = 4


def tree_parents():
    trees = [TREE]
    for _ in range(3):
        trees.append({((-x) % SIDE, z): (-s, d) for (z, x), (d, s) in trees[-1].items()})
    return trees


def children(tree, step):
    return [
        (v[0] - step[0]) % SIDE * SIDE + (v[1] - step[1]) % SIDE
        for v, d in tree.items()
        if d == step
    ]


def depths(tree):
    def depth(v):
        if v == (0, 0):
            return 0
        z, x = v
        d, s = tree[v]
        return 1 + depth(((z - d) % SIDE, (x - s) % SIDE))

    return [depth((v // SIDE, v % SIDE)) for v in range(SIDE * SIDE)]


def one_of(value, options):
    found = value == options[0]
    for other in options[1:]:
        found = found | (value == other)
    return found


def factor_block(x, after_leaf):
    n = x.shape[0]
    leaves = n // 8
    rows = [x[8 * i : 8 * i + 8] for i in range(leaves)]
    lane = lax.broadcasted_iota(jnp.int32, (8, n), 1)
    sub = lax.broadcasted_iota(jnp.int32, (8, n), 0)
    out = []
    for b in range(leaves):
        o = 8 * b
        c = [jnp.broadcast_to(rows[b][:, o + k : o + k + 1], (8, n)) for k in range(8)]
        inside = (lane >= o) & (lane < o + 8)
        g = jnp.where(inside, jnp.where(lane - o == sub, F(1), F(0)), rows[b])
        r = jnp.zeros_like(g)
        for j in range(8):
            pivot = jnp.broadcast_to(c[j][j : j + 1], (8, n))
            inv = 1.0 / pivot
            row = jnp.broadcast_to(g[j : j + 1], (8, n))
            here = sub == j
            r = jnp.where(here, row * lax.rsqrt(pivot), r)
            grow = row * inv
            g = jnp.where(here, grow, g - c[j] * grow)
            for k in range(j + 1, 8):
                ck = jnp.broadcast_to(c[k][j : j + 1], (8, n)) * inv
                c[k] = jnp.where(here, ck, c[k] - c[j] * ck)
        out.append(r)
        if b + 1 < leaves:
            below = rows[b + 1]
            acc = jnp.where(inside, F(0), below)
            for k in range(8):
                acc = acc - jnp.broadcast_to(below[:, o + k : o + k + 1], (8, n)) * jnp.broadcast_to(
                    g[k : k + 1], (8, n)
                )
            rows[b + 1] = acc
        if b + 2 < leaves:
            rest = jnp.concatenate(rows[b + 2 :], axis=0)
            parts = [g, jnp.zeros((n - o - 8, n), F)]
            if o:
                parts = [jnp.zeros((o, n), F)] + parts
            lanes = lax.broadcasted_iota(jnp.int32, rest.shape, 1)
            cleared = jnp.where((lanes >= o) & (lanes < o + 8), F(0), rest)
            rest = cleared - jnp.dot(rest, jnp.concatenate(parts, axis=0), precision=HI, preferred_element_type=F)
            for i in range(b + 2, leaves):
                rows[i] = rest[8 * (i - b - 2) : 8 * (i - b - 2) + 8]
        after_leaf()
    return jnp.concatenate(out, axis=0)


def factor_all(d_ref, w_ref, after_leaf, after_first):
    n = w_ref.shape[0]
    li = lax.broadcasted_iota(jnp.int32, (SB, SB), 1)
    si = lax.broadcasted_iota(jnp.int32, (SB, SB), 0)
    for r0 in range(0, n, SB):
        src = w_ref if r0 else d_ref
        here = pl.ds(r0, SB)
        f = factor_block(src[here, here], after_leaf)
        if not r0:
            after_first()
        w = jnp.where(li <= si, f, F(0))
        w_ref[here, :] = jnp.dot(w, src[here, :], precision=HI, preferred_element_type=F)
        w_ref[here, here] = w
        k0 = r0 + SB
        if k0 < n:
            rr = w_ref[here, :]
            upd = lax.dot_general(
                rr[:, k0:], rr, (((0,), (0,)), ((), ())), precision=HI, preferred_element_type=F
            )
            col = lax.broadcasted_iota(jnp.int32, (n - k0, n), 1)
            old = jnp.where((col >= r0) & (col < k0), F(0), src[pl.ds(k0, n - k0), :])
            w_ref[pl.ds(k0, n - k0), :] = old - upd
            w_ref[here, pl.ds(k0, n - k0)] = jnp.zeros((SB, n - k0), F)


def gather_kernel(
    x_ref, a_ref, t_ref, r_ref, w_ref, d_ref,
    sem_local, sem_stage, t_send, t_recv, r_send, r_recv, s_send, s_recv, d_send, d_recv, h_send, h_recv,
):
    p = lax.axis_index("prow")
    q = lax.axis_index("pcol")
    z, x = p // SIDE, p % SIDE
    y, c = q // 2, q % 2
    tiles = x_ref.shape[3]
    row_tiles = x_ref.shape[0]

    def dev(dz=0, dx=0, dy=0, other=False):
        cc = 1 - c if other else c
        return {
            "prow": (z + dz + SIDE) % SIDE * SIDE + (x + dx + SIDE) % SIDE,
            "pcol": (y + dy + SIDE) % SIDE * 2 + cc,
        }

    partner = dev(other=True)

    stage = []

    def bring(cond, src, dst):
        stage.append((cond, pltpu.make_async_copy(src, dst, sem_stage.at[len(stage)])))

    for row, col in ((0, 0), (0, 1), (1, 1)):
        bring(
            (p == row) & (q == col),
            x_ref.at[0, 0, :, 0, 0, :],
            d_ref.at[pl.ds(NB * row, NB), pl.ds(NB * col, NB)],
        )
    for k in range(2):
        for j in range(tiles):
            bring(p == k, x_ref.at[0, 0, :, j, 0, :], t_ref.at[pl.ds(NB * k, NB), pl.ds(NB * j, NB)])
    for k in range(2):
        for i in range(row_tiles):
            bring(q == k, x_ref.at[i, 0, :, 0, 0, :], r_ref.at[k, pl.ds(NB * i, NB), :])
    for cond, copy in stage:
        pl.when(cond)(copy.start)
    own = [
        pltpu.make_async_copy(
            x_ref.at[i, 0, :, j, 0, :],
            a_ref.at[pl.ds(NB * i, NB), pl.ds(NB * j, NB)],
            sem_local.at[i * tiles + j],
        )
        for i in range(row_tiles)
        for j in range(tiles)
    ]

    barrier = pltpu.get_barrier_semaphore()
    peers = [partner]
    for s in range(1, SIDE):
        peers += [dev(dz=s), dev(dx=s), dev(dy=s)]
    for peer in peers:
        pl.semaphore_signal(barrier, inc=1, device_id=peer, device_id_type=MESH)
    pl.semaphore_wait(barrier, len(peers))
    for cond, copy in stage:
        pl.when(cond)(copy.wait)

    def remote(ref, send, recv, peer):
        return pltpu.make_async_remote_copy(
            src_ref=ref, dst_ref=ref, send_sem=send, recv_sem=recv, device_id=peer, device_id_type=MESH
        )

    sends = []

    def send(cond, copy):
        pl.when(cond)(copy.start)
        sends.append((cond, copy))

    pieces = [
        (0, 128, 0, 128, 0, 0, 0, 0),
        (0, 128, 128, 256, 0, 0, 0, 1),
        (0, 128, 256, 512, 0, 1, 1, 0),
        (128, 256, 128, 256, 0, 0, 0, 2),
        (128, 256, 256, 512, 0, 1, 1, 1),
        (256, 384, 256, 512, 1, 0, 1, 2),
        (384, 512, 384, 512, 1, 0, 1, 3),
    ]
    assert len(pieces) == LEAD

    def piece(i):
        ra, rb, ca, cb = pieces[i][:4]
        ref = d_ref.at[pl.ds(ra, rb - ra), pl.ds(ca, cb - ca)]
        return lambda j, peer: remote(ref, d_send.at[i, j], d_recv.at[i], peer)

    def handed(i):
        return pieces[i][5] != pieces[i][6]

    def root_chip(i):
        return (z == 0) & (x == pieces[i][4]) & (y == 0)

    def hand(i):
        if handed(i):
            send(root_chip(i) & (c == pieces[i][6]), piece(i)(9, partner))

    def lead(i, s):
        x0, c0, owner, begin = pieces[i][4:]
        copy = piece(i)
        mine = c == c0
        rx = (x - x0 + SIDE) % SIDE
        on_y = (z == 0) & (rx == 0)
        place = jnp.where(rx != 0, 3, jnp.where(z != 0, 2, jnp.where(y != 0, 1, 0)))
        k = s - begin - LAG_LEAD * place

        @pl.when(mine & (k == 0))
        def _():
            @pl.when(place != 0 if c0 == owner else place >= 0)
            def _():
                copy(0, partner).wait_recv()

            for step in range(1, SIDE):
                pl.when(on_y & (y == 0))(copy(step - 1, dev(dy=step)).start)
                pl.when((rx == 0) & (z == 0))(copy(step + 2, dev(dz=step)).start)
                pl.when(rx == 0)(copy(step + 5, dev(dx=step)).start)
            if c0 == owner:
                copy(9, partner).start()
            else:
                pl.when(place != 0)(copy(9, partner).start)

        @pl.when(jnp.logical_not(mine) & (k == 1))
        def _():
            pl.when((place != 0) if c0 != owner else (place >= 0))(copy(9, partner).wait_recv)

    def lead_sent(i):
        x0, c0, owner, _ = pieces[i][4:]
        copy = piece(i)
        mine = c == c0
        rx = (x - x0 + SIDE) % SIDE
        home = (z == 0) & (rx == 0) & (y == 0)

        @pl.when(mine)
        def _():
            for step in range(1, SIDE):
                pl.when(home)(copy(step - 1, dev(dy=step)).wait_send)
                pl.when((rx == 0) & (z == 0))(copy(step + 2, dev(dz=step)).wait_send)
                pl.when(rx == 0)(copy(step + 5, dev(dx=step)).wait_send)
            if c0 == owner:
                copy(9, partner).wait_send()
            else:
                pl.when(jnp.logical_not(home))(copy(9, partner).wait_send)

    half = row_tiles * NB // 2
    piece_rows = half // ROW_CHUNKS

    def row_copy(down, i, j, peer):
        ref = r_ref.at[c, pl.ds(pl.multiple_of(down * half + i * piece_rows, piece_rows), piece_rows), :]
        recv = s_recv.at[0] if j == 1 else r_recv.at[down, i]
        return remote(ref, (s_send if j == 1 else r_send).at[down, i], recv, peer)

    def row_each(s, action):
        for down in range(2):
            far = (SIDE - y) % SIDE if down else y
            since = s - ROW_START - LAG * far
            i = since // EVERY
            pl.when((since >= 0) & (since % EVERY == 0) & (i < ROW_CHUNKS))(functools.partial(action, down, i, far))

    def row_pass(down, i, far):
        peer = dev(dy=SIDE - 1 if down else 1)
        pl.when(far != 0)(row_copy(down, i, 0, peer).wait_recv)
        pl.when(far != SIDE - 1)(row_copy(down, i, 0, peer).start)
        row_copy(down, i, 1, partner).start()

    def row_sent(down, i, far):
        peer = dev(dy=SIDE - 1 if down else 1)
        pl.when(far != SIDE - 1)(row_copy(down, i, 0, peer).wait_send)
        row_copy(down, i, 1, partner).wait_send()

    trees = tree_parents()
    rel = [z * SIDE + (x - k + SIDE) % SIDE for k in range(2)]
    has = [[[one_of(rel[k], children(t, s)) for s in STEPS] for t in trees] for k in range(2)]
    deep = [depths(t) for t in trees]
    depth = [
        [sum(jnp.where(rel[k] == v, d, 0) for v, d in enumerate(deep[t])) for t in range(len(trees))]
        for k in range(2)
    ]
    most = max(max(d) for d in deep)
    share = NB // len(trees)
    count = share // 8 * SPLIT
    wide = t_ref.shape[1] // SPLIT
    peer4 = [dev(dz=dz, dx=dx) for dz, dx in STEPS]

    def hop(k, t, i, j):
        e = k * len(trees) + t
        start = pl.multiple_of(NB * k + share * t + i // SPLIT * 8, 8)
        ref = t_ref.at[pl.ds(start, 8), pl.ds(pl.multiple_of(i % SPLIT * wide, wide), wide)]
        return remote(ref, t_send.at[e, i, j], t_recv.at[e, i], peer4[j])

    def tree_each(s, action):
        for k in range(2):
            for t in range(len(trees)):
                since = s - k - LAG * depth[k][t]
                i = since // EVERY
                pl.when((since >= 0) & (since % EVERY == 0) & (i < count))(functools.partial(action, k, t, i))

    def forward(k, t, i):
        pl.when(depth[k][t] != 0)(hop(k, t, i, 0).wait_recv)
        for j in range(len(STEPS)):
            pl.when(has[k][t][j])(hop(k, t, i, j).start)

    def sent(k, t, i):
        for j in range(len(STEPS)):
            pl.when(has[k][t][j])(hop(k, t, i, j).wait_send)

    last_lead = max(v[7] for v in pieces) + 3 * LAG_LEAD + 1
    last_row = ROW_START + EVERY * (ROW_CHUNKS - 1) + LAG * (SIDE - 1)
    last_tree = EVERY * (count - 1) + LAG * most + 1
    steps = 1 + max(last_tree, last_lead, last_row)

    def wave(s):
        for i in range(len(pieces)):
            if not isinstance(s, int) or pieces[i][7] <= s <= pieces[i][7] + 3 * LAG_LEAD + 1:
                lead(i, s)
        if not isinstance(s, int) or s <= last_row:
            row_each(s, row_pass)
        tree_each(s, forward)

    for i in range(len(pieces)):
        hand(i)

    def early(s, carry):
        wave(s)
        return carry

    first_wave = 3 * LAG_LEAD + 2
    lax.fori_loop(0, 2, early, 0)
    for copy in own:
        copy.start()
    lax.fori_loop(2, first_wave, early, 0)
    later = list(range(first_wave, steps))
    leaf = [0]

    def after_leaf():
        leaf[0] += 1
        if leaf[0] % PACE == 0 and later:
            wave(later.pop(0))

    def after_first():
        while later and later[0] <= last_lead:
            wave(later.pop(0))

    factor_all(d_ref, w_ref, after_leaf, after_first)
    while later:
        wave(later.pop(0))
    ref = r_ref.at[1 - c]
    remote(ref, s_send.at[0, 0], s_recv.at[0], partner).wait_recv()

    def drain(s, carry):
        tree_each(s, sent)
        row_each(s, row_sent)
        return carry

    lax.fori_loop(0, steps, drain, 0)
    for i in range(len(pieces)):
        lead_sent(i)
    for cond, copy in sends:
        pl.when(cond)(copy.wait_send)
    for copy in own:
        copy.wait()


def split(v):
    hi = v.astype(BF)
    return hi, (v - hi.astype(F)).astype(BF)


def dot(a, b):
    return jnp.dot(a, b, preferred_element_type=F)


def exact(a, b, dims=(((1,), (0,)), ((), ()))):
    return lax.dot_general(a, b, dims, precision=HI, preferred_element_type=F)


def update_kernel(a_ref, t_ref, r_ref, w_ref, o_ref, pan, bhi, blo, buf, sem):
    p = lax.axis_index("prow")
    q = lax.axis_index("pcol")
    tiles = a_ref.shape[1] // NB
    row_tiles = a_ref.shape[0] // NB
    across = (((1,), (1,)), ((), ()))
    w00 = w_ref[:NB, :NB]
    w1 = w_ref[NB:, :]
    w11 = w_ref[NB:, NB:]
    r0, r1 = r_ref[0], r_ref[1]
    pan[0] = exact(r0, w00, across)
    pan[1] = exact(r0, w1[:, :NB], across) + exact(r1, w11, across)
    for k, v in ((0, exact(pan[0], w00) + exact(pan[1], w1[:, :NB])), (1, exact(pan[1], w11))):
        hi, lo = split(v)
        bhi[:, NB * k : NB * k + NB] = hi
        blo[:, NB * k : NB * k + NB] = lo

    def copy(j, i):
        return pltpu.make_async_copy(
            buf.at[j % 2, pl.ds(NB * i, NB), :], o_ref.at[i, 0, :, j, 0, :], sem.at[j % 2, i]
        )

    def body(j, carry):
        sl = pl.ds(pl.multiple_of(j * NB, NB), NB)
        hi, lo = split(t_ref[:, sl])

        @pl.when(j >= 2)
        def _():
            for i in range(row_tiles):
                copy(j - 2, i).wait()

        for i in range(row_tiles):
            rows = slice(NB * i, NB * i + NB)
            h, l = bhi[rows, :], blo[rows, :]
            buf[j % 2, rows, :] = a_ref[rows, sl] - (dot(h, hi) + (dot(h, lo) + dot(l, hi)))

        @pl.when(p <= 1)
        def _():
            buf[j % 2, :NB, :] = jnp.zeros((NB, NB), F)

        for k in range(2):

            @pl.when((j == 0) & (q == k))
            def _():
                buf[0] = pan[k]
                ri = lax.broadcasted_iota(jnp.int32, (NB, NB), 0)
                ci = lax.broadcasted_iota(jnp.int32, (NB, NB), 1)
                keep = (p > k) | ((p == k) & (ci <= ri))
                buf[0, :NB, :] = jnp.where(keep, pan[k, :NB, :], F(0))

        for i in range(row_tiles):
            copy(j, i).start()
        return carry

    lax.fori_loop(0, tiles, body, 0)
    for j in range(tiles - 2, tiles):
        for i in range(row_tiles):
            copy(j, i).wait()


def shards(kernel_tiles):
    row_tiles, _, nb, tiles, _, _ = kernel_tiles.shape
    rows, cols, lead = row_tiles * nb, tiles * nb, 2 * nb
    vmem = pl.BlockSpec(memory_space=pltpu.VMEM)
    dma = pltpu.SemaphoreType.DMA
    count = nb // 4 // 8 * SPLIT
    a, t, r, w = pl.pallas_call(
        gather_kernel,
        out_shape=[
            jax.ShapeDtypeStruct((rows, cols), F),
            jax.ShapeDtypeStruct((lead, cols), F),
            jax.ShapeDtypeStruct((2, rows, nb), F),
            jax.ShapeDtypeStruct((lead, lead), F),
        ],
        in_specs=[pl.BlockSpec(memory_space=pltpu.HBM)],
        out_specs=[vmem] * 4,
        scratch_shapes=[
            pltpu.VMEM((lead, lead), F),
            dma((row_tiles * tiles,)),
            dma((2 * tiles + 3 + 2 * row_tiles,)),
            dma((8, count, 4)),
            dma((8, count)),
            dma((2, ROW_CHUNKS)),
            dma((2, ROW_CHUNKS)),
            dma((2, ROW_CHUNKS)),
            dma((1,)),
            dma((LEAD, 10)),
            dma((LEAD,)),
            dma((1,)),
            dma((1,)),
        ],
        compiler_params=pltpu.CompilerParams(
            collective_id=0, has_side_effects=True, vmem_limit_bytes=32 * 2**20
        ),
        name="gather_and_factor",
    )(kernel_tiles)
    return pl.pallas_call(
        update_kernel,
        out_shape=jax.ShapeDtypeStruct(kernel_tiles.shape, F),
        in_specs=[vmem] * 4,
        out_specs=pl.BlockSpec(memory_space=pl.ANY),
        scratch_shapes=[
            pltpu.VMEM((2, rows, nb), F),
            pltpu.VMEM((rows, lead), BF),
            pltpu.VMEM((rows, lead), BF),
            pltpu.VMEM((2, rows, nb), F),
            dma((2, row_tiles)),
        ],
        compiler_params=pltpu.CompilerParams(vmem_limit_bytes=28 * 2**20),
        name="update",
    )(a, t, r, w)


def solution(mesh):
    spec = P(None, "prow", None, None, "pcol", None)
    return jax.shard_map(shards, mesh=mesh, in_specs=(spec,), out_specs=spec, check_vma=False)
```

time: 159 us -> 90.9 us (0.57)
  the two profiles are of different devices: /device:TPU:88 before, /device:TPU:35 now
where the time goes in v3:
time: 90.9 us; the launch traced here: 90.8 us
  Pallas kernels  90.6 us (100%)
    pallas_call x1, Pallas kernels, shards(): pl.pallas_call(gather_kernel, out_shape=[jax.ShapeDtypeStruct((rows, cols...  73.8 us
    pallas_call x1, Pallas kernels, shards(): pl.pallas_call(update_kernel, out_shape=jax.ShapeDtypeStruct(kernel_tiles...  16.8 us

profile of v3, /device:TPU:35, one launch (start us, length us, event | category | flops | bytes accessed | tf_op | source)
XLA Modules:
  0.0 90.8 jit_solution(882382214382363767)
XLA Ops:
  0.0 73.8 %gather_and_factor.1 = (f32[1024,2048]{1,0:T(8,128)S(1)}, f32[512,2048]{1,0:T(8,128)S(1)}, f32[2,1024,256]{2,1,0:T(8,128)S(1)}, f32[512,512]{1,0:T(8,128)S(1)}) custom-call(f32[4,1,256,8,1,256]{5,4,3,2,1,0:T(1,128)} %x_ref.1), custom_call_target="tpu_custom_call" | custom-call | tf_op jit(solution)/shard_map/gather_and_factor/pallas_call | solution.py:479
  73.8 16.8 %update.1 = f32[4,1,256,8,1,256]{5,4,3,2,1,0:T(1,128)} custom-call(f32[1024,2048]{1,0:T(8,128)S(1)} %get-tuple-element.9.a_ref, f32[512,2048]{1,0:T(8,128)S(1)} %get-tuple-element.10.t_ref, f32[2,1024,256]{2,1,0:T(8,128)S(1)} %get-tuple-element.11.r_ref, f32[512,512]{1,0:T(8,128)S(1)} %get-tuple-element.12.w_ref), custom_call_target="tpu_custom_call" | custom-call | tf_op jit(solution)/shard_map/update/pallas_call | solution.py:509

commit v4 on v3

--- a/solution.py
+++ b/solution.py
@@ -26,8 +26,7 @@
 LEAD = 7
 ROW_CHUNKS = 4
 ROW_START = 2
-EVERY = 1
-SPLIT = 1
+TREE_START = 5
 PACE = 4
 
 
@@ -284,14 +283,13 @@
     def row_copy(down, i, j, peer):
         ref = r_ref.at[c, pl.ds(pl.multiple_of(down * half + i * piece_rows, piece_rows), piece_rows), :]
         recv = s_recv.at[0] if j == 1 else r_recv.at[down, i]
-        return remote(ref, (s_send if j == 1 else r_send).at[down, i], recv, peer)
+        return remote(ref, (s_send if j == 1 else r_send).at[down], recv, peer)
 
     def row_each(s, action):
         for down in range(2):
             far = (SIDE - y) % SIDE if down else y
-            since = s - ROW_START - LAG * far
-            i = since // EVERY
-            pl.when((since >= 0) & (since % EVERY == 0) & (i < ROW_CHUNKS))(functools.partial(action, down, i, far))
+            i = s - ROW_START - LAG * far
+            pl.when((i >= 0) & (i < ROW_CHUNKS))(functools.partial(action, down, i, far))
 
     def row_pass(down, i, far):
         peer = dev(dy=SIDE - 1 if down else 1)
@@ -299,10 +297,12 @@
         pl.when(far != SIDE - 1)(row_copy(down, i, 0, peer).start)
         row_copy(down, i, 1, partner).start()
 
-    def row_sent(down, i, far):
-        peer = dev(dy=SIDE - 1 if down else 1)
-        pl.when(far != SIDE - 1)(row_copy(down, i, 0, peer).wait_send)
-        row_copy(down, i, 1, partner).wait_send()
+    def rows_sent():
+        for down in range(2):
+            far = (SIDE - y) % SIDE if down else y
+            ref = r_ref.at[c, pl.ds(down * half, half), :]
+            pl.when(far != SIDE - 1)(remote(ref, r_send.at[down], r_recv.at[down, 0], partner).wait_send)
+            remote(ref, s_send.at[down], s_recv.at[0], partner).wait_send()
 
     trees = tree_parents()
     rel = [z * SIDE + (x - k + SIDE) % SIDE for k in range(2)]
@@ -314,35 +314,37 @@
     ]
     most = max(max(d) for d in deep)
     share = NB // len(trees)
-    count = share // 8 * SPLIT
-    wide = t_ref.shape[1] // SPLIT
+    count = share // 8
+    begin = [[TREE_START + LAG * d for d in row] for row in depth]
     peer4 = [dev(dz=dz, dx=dx) for dz, dx in STEPS]
 
     def hop(k, t, i, j):
         e = k * len(trees) + t
-        start = pl.multiple_of(NB * k + share * t + i // SPLIT * 8, 8)
-        ref = t_ref.at[pl.ds(start, 8), pl.ds(pl.multiple_of(i % SPLIT * wide, wide), wide)]
-        return remote(ref, t_send.at[e, i, j], t_recv.at[e, i], peer4[j])
+        ref = t_ref.at[pl.ds(pl.multiple_of(NB * k + share * t + i * 8, 8), 8), :]
+        return remote(ref, t_send.at[e, j], t_recv.at[e, i], peer4[j])
 
     def tree_each(s, action):
         for k in range(2):
             for t in range(len(trees)):
-                since = s - k - LAG * depth[k][t]
-                i = since // EVERY
-                pl.when((since >= 0) & (since % EVERY == 0) & (i < count))(functools.partial(action, k, t, i))
+                i = s - begin[k][t]
+                pl.when((i >= 0) & (i < count))(functools.partial(action, k, t, i))
 
     def forward(k, t, i):
         pl.when(depth[k][t] != 0)(hop(k, t, i, 0).wait_recv)
         for j in range(len(STEPS)):
             pl.when(has[k][t][j])(hop(k, t, i, j).start)
 
-    def sent(k, t, i):
-        for j in range(len(STEPS)):
-            pl.when(has[k][t][j])(hop(k, t, i, j).wait_send)
+    def trees_sent():
+        for k in range(2):
+            for t in range(len(trees)):
+                e = k * len(trees) + t
+                ref = t_ref.at[pl.ds(NB * k + share * t, share), :]
+                for j in range(len(STEPS)):
+                    pl.when(has[k][t][j])(remote(ref, t_send.at[e, j], t_recv.at[e, 0], peer4[j]).wait_send)
 
     last_lead = max(v[7] for v in pieces) + 3 * LAG_LEAD + 1
-    last_row = ROW_START + EVERY * (ROW_CHUNKS - 1) + LAG * (SIDE - 1)
-    last_tree = EVERY * (count - 1) + LAG * most + 1
+    last_row = ROW_START + ROW_CHUNKS - 1 + LAG * (SIDE - 1)
+    last_tree = TREE_START + count - 1 + LAG * most
     steps = 1 + max(last_tree, last_lead, last_row)
 
     def wave(s):
@@ -381,14 +383,10 @@
     while later:
         wave(later.pop(0))
     ref = r_ref.at[1 - c]
-    remote(ref, s_send.at[0, 0], s_recv.at[0], partner).wait_recv()
-
-    def drain(s, carry):
-        tree_each(s, sent)
-        row_each(s, row_sent)
-        return carry
-
-    lax.fori_loop(0, steps, drain, 0)
+    remote(ref, s_send.at[0], s_recv.at[0], partner).wait_recv()
+
+    trees_sent()
+    rows_sent()
     for i in range(len(pieces)):
         lead_sent(i)
     for cond, copy in sends:
@@ -475,7 +473,7 @@
     rows, cols, lead = row_tiles * nb, tiles * nb, 2 * nb
     vmem = pl.BlockSpec(memory_space=pltpu.VMEM)
     dma = pltpu.SemaphoreType.DMA
-    count = nb // 4 // 8 * SPLIT
+    count = nb // 4 // 8
     a, t, r, w = pl.pallas_call(
         gather_kernel,
         out_shape=[
@@ -490,11 +488,11 @@
             pltpu.VMEM((lead, lead), F),
             dma((row_tiles * tiles,)),
             dma((2 * tiles + 3 + 2 * row_tiles,)),
-            dma((8, count, 4)),
+            dma((8, 4)),
             dma((8, count)),
+            dma((2,)),
             dma((2, ROW_CHUNKS)),
-            dma((2, ROW_CHUNKS)),
-            dma((2, ROW_CHUNKS)),
+            dma((2,)),
             dma((1,)),
             dma((LEAD, 10)),
             dma((LEAD,)),

time: 90.9 us -> 80.1 us (0.88)
  the two profiles are of different devices: /device:TPU:35 before, /device:TPU:88 now
where the time goes in v4:
time: 80.1 us; the launch traced here: 79 us
  Pallas kernels  78.8 us (98%)
    pallas_call x1, Pallas kernels, shards(): pl.pallas_call(gather_kernel, out_shape=[jax.ShapeDtypeStruct((rows, cols...  62.1 us
    pallas_call x1, Pallas kernels, shards(): pl.pallas_call(update_kernel, out_shape=jax.ShapeDtypeStruct(kernel_tiles...  16.7 us

profile of v4, /device:TPU:88, one launch (start us, length us, event | category | flops | bytes accessed | tf_op | source)
XLA Modules:
  0.0 79.0 jit_solution(484924765044308684)
XLA Ops:
  0.0 62.1 %gather_and_factor.1 = (f32[1024,2048]{1,0:T(8,128)S(1)}, f32[512,2048]{1,0:T(8,128)S(1)}, f32[2,1024,256]{2,1,0:T(8,128)S(1)}, f32[512,512]{1,0:T(8,128)S(1)}) custom-call(f32[4,1,256,8,1,256]{5,4,3,2,1,0:T(1,128)} %x_ref.1), custom_call_target="tpu_custom_call" | custom-call | tf_op jit(solution)/shard_map/gather_and_factor/pallas_call | solution.py:477
  62.1 16.7 %update.1 = f32[4,1,256,8,1,256]{5,4,3,2,1,0:T(1,128)} custom-call(f32[1024,2048]{1,0:T(8,128)S(1)} %get-tuple-element.9.a_ref, f32[512,2048]{1,0:T(8,128)S(1)} %get-tuple-element.10.t_ref, f32[2,1024,256]{2,1,0:T(8,128)S(1)} %get-tuple-element.11.r_ref, f32[512,512]{1,0:T(8,128)S(1)} %get-tuple-element.12.w_ref), custom_call_target="tpu_custom_call" | custom-call | tf_op jit(solution)/shard_map/update/pallas_call | solution.py:507
